TPU v7x, 256 devices: a whole 4x4x8 slice. The times are simulated.
256 devices in a mesh: section: 8 (over y_hi, x), ctx: 32 (over y_lo, z, core).
Axes of the slice: x: 4, y: 4 (y_hi: 2, y_lo: 2; y = y_hi * 2 + y_lo), z: 8, core: 2. Of those that a mesh axis runs over, the one named last changes fastest.
Arguments:
- projected: bfloat16 [8, 12288, 3072], P('section', 'ctx'), may hold values from -64 to 64
- grad_out: bfloat16 [8, 12288, 3072], P('section', 'ctx'), may hold values from -6 to 6
- doc_lengths: int32 [31], replicated, may hold values from 1 to 768, as said below
Outputs:
- grad_kv: float32 [12288, 2048], P('ctx')
Inputs may be any that keep to these rules, and one draw needn't show every extreme that they name: `doc_lengths`: the lengths sum to 12288; the first document is shorter than 384 tokens and the second has exactly 768.
All inputs are finite; a program needn't handle non-finite values.
Results may differ from a plain program's by a relative error of at most 0.0031.
Values may be sent and summed in bfloat16 or wider, within the bound.
No kernel may reach another device: no remote copies, remote signals or barrier semaphores. Data moves between devices by JAX's collectives and lax.ppermute only.
A program may use at most 128 MiB of HBM per device.

v0:
```python
import math
import jax
import jax.numpy as jnp
from jax import lax
from jax.sharding import PartitionSpec as P

HEAD_SIZE = 128
KV_HEAD_COUNT = 8
QUERY_PER_KV = 3
REACH = 2
MASKED_SCORE = -1e30


def spread(value, axis, source):
    kept = jnp.where(lax.axis_index(axis) == source, value, 0).astype(value.dtype)
    return lax.psum(kept, axis)


def shifted(value, axis, steps):
    count = lax.axis_size(axis)
    leading, last = (max(0, -steps), min(count, count - steps))
    return lax.ppermute(value, axis, [(source, source + steps) for source in range(leading, last)])


def document_of(places, doc_ends):
    return jnp.sum((doc_ends[None, :] <= places[:, None]).astype(jnp.int32), axis=1)


def piece_scores(query_group, key_part, piece_mask, score_scale):
    scores = (
        jnp.einsum("qah,kh->aqk", query_group, key_part, preferred_element_type=jnp.float32)
        * score_scale
    )
    return jnp.where(piece_mask[None], scores, MASKED_SCORE)


def piece_attend(weight_part, value_part):
    return jnp.einsum("aqk,kh->qah", weight_part, value_part, preferred_element_type=jnp.float32)


def piece_grads(
    prob_part, weight_part, query_group, grad_group, value_part, delta_rows, score_scale
):
    grad_value = jnp.einsum(
        "aqk,qah->kh", weight_part, grad_group, preferred_element_type=jnp.float32
    )
    grad_prob = jnp.einsum(
        "qah,kh->aqk", grad_group, value_part, preferred_element_type=jnp.float32
    )
    grad_score = (prob_part * (grad_prob - delta_rows)).astype(jnp.bfloat16)
    grad_key = (
        jnp.einsum("aqk,qah->kh", grad_score, query_group, preferred_element_type=jnp.float32)
        * score_scale
    )
    return (grad_key, grad_value)


def on_device(projected, grad_out, doc_lengths):
    tok_rows = projected.shape[1]
    head_dim = HEAD_SIZE
    shared_key_heads = KV_HEAD_COUNT
    group = QUERY_PER_KV
    shared_width = shared_key_heads * head_dim
    out_width = 2 * shared_width
    reaching = REACH
    pieces = reaching + 1
    score_scale = 1.0 / math.sqrt(head_dim)
    shared = spread(projected[0][:, :out_width], "section", 0)
    earlier = []
    for distance in range(reaching, 0, -1):
        earlier.append(shifted(shared, "ctx", distance))
    window = jnp.concatenate(earlier + [shared], axis=0)
    key_heads = window[:, :shared_width].reshape(pieces * tok_rows, shared_key_heads, head_dim)
    value_heads = window[:, shared_width:].reshape(pieces * tok_rows, shared_key_heads, head_dim)
    queries = projected[0].reshape(tok_rows, shared_key_heads, group, head_dim)
    grad_heads = grad_out[0].reshape(tok_rows, shared_key_heads, group, head_dim)
    doc_ends = jnp.cumsum(doc_lengths)
    ctx_index = lax.axis_index("ctx")
    query_place = ctx_index * tok_rows + jnp.arange(tok_rows, dtype=jnp.int32)
    key_place = (ctx_index - reaching) * tok_rows + jnp.arange(pieces * tok_rows, dtype=jnp.int32)
    same_doc = (
        document_of(query_place, doc_ends)[:, None] == document_of(key_place, doc_ends)[None, :]
    )
    allowed = same_doc & (key_place[None, :] <= query_place[:, None]) & (key_place[None, :] >= 0)

    def group_grads(kv_index):
        query_group = lax.dynamic_index_in_dim(queries, kv_index, 1, keepdims=False)
        grad_group = lax.dynamic_index_in_dim(grad_heads, kv_index, 1, keepdims=False)
        key_group = lax.dynamic_index_in_dim(key_heads, kv_index, 1, keepdims=False)
        value_group = lax.dynamic_index_in_dim(value_heads, kv_index, 1, keepdims=False)
        score_parts = []
        for index in range(pieces):
            rows = slice(index * tok_rows, (index + 1) * tok_rows)
            score_parts.append(
                piece_scores(query_group, key_group[rows], allowed[:, rows], score_scale)
            )
        scores = jnp.concatenate(score_parts, axis=2)
        row_top = jnp.max(scores, axis=2, keepdims=True)
        powers = jnp.exp(scores - row_top)
        attn_weight = powers / jnp.sum(powers, axis=2, keepdims=True)
        attn_half = attn_weight.astype(jnp.bfloat16)
        attended = jnp.zeros((tok_rows, group, head_dim), jnp.float32)
        for index in range(pieces):
            rows = slice(index * tok_rows, (index + 1) * tok_rows)
            attended = attended + piece_attend(attn_half[:, :, rows], value_group[rows])
        delta_rows = jnp.sum(grad_group.astype(jnp.float32) * attended, axis=2).T[:, :, None]
        key_parts = []
        value_parts = []
        for index in range(pieces):
            rows = slice(index * tok_rows, (index + 1) * tok_rows)
            grad_key, grad_value = piece_grads(
                attn_weight[:, :, rows],
                attn_half[:, :, rows],
                query_group,
                grad_group,
                value_group[rows],
                delta_rows,
                score_scale,
            )
            key_parts.append(grad_key)
            value_parts.append(grad_value)
        return (jnp.concatenate(key_parts, axis=0), jnp.concatenate(value_parts, axis=0))

    key_grads, value_grads = lax.map(group_grads, jnp.arange(shared_key_heads, dtype=jnp.int32))
    is_cross = (lax.axis_index("section") > 0).astype(jnp.float32)
    key_flat = jnp.transpose(key_grads, (1, 0, 2)).reshape(pieces * tok_rows, shared_width)
    value_flat = jnp.transpose(value_grads, (1, 0, 2)).reshape(pieces * tok_rows, shared_width)
    grad_pieces = (jnp.concatenate([key_flat, value_flat], axis=1) * is_cross).reshape(
        pieces, tok_rows, out_width
    )
    summed = grad_pieces[reaching]
    for distance in range(1, reaching + 1):
        summed = summed + shifted(grad_pieces[reaching - distance], "ctx", -distance)
    return lax.psum(summed, "section")


def solution(mesh):
    return jax.shard_map(
        on_device,
        mesh=mesh,
        in_specs=(P("section", "ctx", None), P("section", "ctx", None), P()),
        out_specs=P("ctx", None),
        check_vma=False,
    )
```

profile of v0, /device:TPU:32, one launch (start us, length us, event | category | flops | bytes accessed | tf_op | source)
XLA Modules:
  0.0 628.3 jit_solution(13634412280099903388)
XLA Ops:
  6.5 4.3 copy.56
  10.8 2.9 slice_select_fusion
  13.8 97.9 %all-reduce.3.cloned.1.call-done = bf16[384,2048]{0,1:T(8,128)(2,1)} async-done(((bf16[384,2048]{0,1:T(8,128)(2,1)}), bf16[384,2048]{0,1:T(8,128)(2,1)}) %all-reduce.3.cloned.1.call-update) | async-done | bytes 1572880 | tf_op jit(solution)/shard_map/psum | solution.py:16
  111.6 3.5 collective-permute-start
  117.3 2.4 copy.58
  122.0 29.1 %collective-permute-done = bf16[384,2048]{0,1:T(8,128)(2,1)} collective-permute-done((bf16[384,2048]{0,1:T(8,128)(2,1)}, bf16[384,2048]{0,1:T(8,128)(2,1)}, u32[]{:S(2)}, u32[]{:S(2)}) %collective-permute-start) | collective-permute-done | bytes 1572896 | tf_op jit(solution)/shard_map/ppermute | solution.py:22
  152.7 8.9 %collective-permute-done.1 = bf16[384,2048]{0,1:T(8,128)(2,1)} collective-permute-done((bf16[384,2048]{0,1:T(8,128)(2,1)}, bf16[384,2048]{0,1:T(8,128)(2,1)}, u32[]{:S(2)}, u32[]{:S(2)}) %collective-permute-start.1) | collective-permute-done | bytes 1572896 | tf_op jit(solution)/shard_map/ppermute | solution.py:22
  163.6 2.5 fusion.71
  166.1 224.7 %while.12 = (s32[]{:T(128)}, f32[8,1152,128]{2,1,0:T(8,128)}, f32[8,1152,128]{2,1,0:T(8,128)}, pred[384,1152]{0,1:T(8,128)(4,1)}, s32[8]{0:T(128)S(1)}, /*index=...) while((s32[]{:T(128)}, f32[8,1152,128]{2,1,0:T(8,128)}, ...), condition=%wide.region_10.11_spmd, body=%wide.region_4.10_spmd.sunk | while | flops 1720070784 | bytes 68940056 | solution.py:124
  175.2 3.7 fusion.121
  187.2 2.4 fusion.125
  203.3 3.7 fusion.121
  215.2 2.4 fusion.125
  231.3 3.7 fusion.121
  243.3 2.4 fusion.125
  259.5 3.7 fusion.121
  271.4 2.4 fusion.125
  287.5 3.7 fusion.121
  299.5 2.4 fusion.125
  315.6 3.7 fusion.121
  327.6 2.4 fusion.125
  343.7 3.7 fusion.121
  355.7 2.4 fusion.125
  371.8 3.7 fusion.121
  383.8 2.4 fusion.125
  390.8 8.7 %copy_bitcast_fusion = (f32[1152,1024]{1,0:T(8,128)}, f32[1152,1024]{1,0:T(8,128)}) fusion(f32[8,1152,128]{2,1,0:T(8,128)} %get-tuple-element.53, f32[8,1152,128]{2,1,0:T(8,128)} %get-tuple-element.54), kind=kLoop, calls=%fused_computation.83 | loop fusion | bytes 18874368 | tf_op jit(solution)/shard_map/reshape | solution.py:127
  399.5 4.9 maximum_multiply_fusion
  409.0 64.8 %collective-permute-done.2 = f32[384,2048]{1,0:T(8,128)S(1)} collective-permute-done((f32[384,2048]{1,0:T(8,128)S(1)}, f32[384,2048]{1,0:T(8,128)S(1)}, u32[]{:S(2)}, u32[]{:S(2)}) %collective-permute-start.2) | collective-permute-done | bytes 3145760 | tf_op jit(solution)/shard_map/ppermute | solution.py:22
  473.8 37.5 %collective-permute-done.3 = f32[384,2048]{1,0:T(8,128)S(1)} collective-permute-done((f32[384,2048]{1,0:T(8,128)S(1)}, f32[384,2048]{1,0:T(8,128)S(1)}, u32[]{:S(2)}, u32[]{:S(2)}) %collective-permute-start.3) | collective-permute-done | bytes 3145760 | tf_op jit(solution)/shard_map/ppermute | solution.py:22
  511.2 2.7 fusion.63
  513.9 103.6 %all-reduce.5.cloned.1.call-done = f32[384,2048]{1,0:T(8,128)} async-done(((f32[384,2048]{1,0:T(8,128)}), f32[384,2048]{1,0:T(8,128)}) %all-reduce.5.cloned.1.call-update) | async-done | bytes 3145744 | tf_op jit(solution)/shard_map/psum | solution.py:134
  617.5 3.9 copy.108
  (205 shorter events, 172.0 us)
Async XLA Ops:
  6.5 105.1 %all-reduce.3.cloned.1.call-start = ((), (), s32[]{:S(2)}) async-start(), calls=%async_computation | async-start | bytes 3145728 | tf_op jit(solution)/shard_map/psum | solution.py:16
  10.8 106.2 %copy-start.4 = (s32[31]{0:T(128)S(1)}, s32[31]{0:T(128)}, u32[]{:S(2)}) copy-start(s32[31]{0:T(128)} %param.7) | copy-start | bytes 376
  10.8 106.5 %copy-start.2 = (bf16[1,384,3072]{2,1,0:T(8,128)(2,1)S(1)}, bf16[1,384,3072]{2,1,0:T(8,128)(2,1)}, u32[]{:S(2)}) copy-start(bf16[1,384,3072]{2,1,0:T(8,128)(2,1)} %param.6) | copy-start | bytes 7077892
  13.7 603.8 %all-reduce.5.cloned.1.call-start = ((), (), s32[]{:S(2)}) async-start(), calls=%async_computation.1 | async-start | bytes 6291456 | tf_op jit(solution)/shard_map/psum | solution.py:134
  111.6 39.5 %collective-permute-start = (bf16[384,2048]{0,1:T(8,128)(2,1)}, bf16[384,2048]{0,1:T(8,128)(2,1)}, u32[]{:S(2)}, u32[]{:S(2)}) collective-permute-start(bf16[384,2048]{0,1:T(8,128)(2,1)} %all-reduce.3.cloned.1.call-done), channel_id=1, source_target_pairs={{0,2},{1,3},{2,4},{3,5},{4,6},{5,7},{6,8},{7,9},{8,10},{9,11},{10,... | collective-permute-start | bytes 4718600 | tf_op jit(solution)/shard_map/ppermute | solution.py:22
  115.1 46.4 %collective-permute-start.1 = (bf16[384,2048]{0,1:T(8,128)(2,1)}, bf16[384,2048]{0,1:T(8,128)(2,1)}, u32[]{:S(2)}, u32[]{:S(2)}) collective-permute-start(bf16[384,2048]{0,1:T(8,128)(2,1)} %all-reduce.3.cloned.1.call-done), channel_id=1, source_target_pairs={{0,1},{1,2},{2,3},{3,4},{4,5},{5,6},{6,7},{7,8},{8,9},{9,10},{10,1... | collective-permute-start | bytes 4718600 | tf_op jit(solution)/shard_map/ppermute | solution.py:22
  122.0 41.2 %copy-start.3 = (bf16[384,2048]{0,1:T(8,128)(2,1)S(1)}, bf16[384,2048]{0,1:T(8,128)(2,1)}, u32[]{:S(2)}) copy-start(bf16[384,2048]{0,1:T(8,128)(2,1)} %all-reduce.3.cloned.1.call-done) | copy-start | bytes 4718596
  178.9 1.5 copy-start
  187.2 4.7 copy-start.1
  207.0 1.5 copy-start
  215.2 4.7 copy-start.1
  235.0 1.5 copy-start
  243.3 4.7 copy-start.1
  263.2 1.5 copy-start
  271.4 4.7 copy-start.1
  291.2 1.5 copy-start
  299.5 4.7 copy-start.1
  319.3 1.5 copy-start
  327.6 4.7 copy-start.1
  347.4 1.5 copy-start
  355.7 4.7 copy-start.1
  375.5 1.5 copy-start
  383.8 4.7 copy-start.1
  405.1 68.7 %collective-permute-start.2 = (f32[384,2048]{1,0:T(8,128)S(1)}, f32[384,2048]{1,0:T(8,128)S(1)}, u32[]{:S(2)}, u32[]{:S(2)}) collective-permute-start(f32[384,2048]{1,0:T(8,128)S(1)} %get-tuple-element.113), channel_id=1, source_target_pairs={{1,0},{2,1},{3,2},{4,3},{5,4},{6,5},{7,6},{8,7},{9,8},{10,9},{11,1... | collective-permute-start | bytes 9437192 | tf_op jit(solution)/shard_map/ppermute | solution.py:22
  407.0 104.2 %collective-permute-start.3 = (f32[384,2048]{1,0:T(8,128)S(1)}, f32[384,2048]{1,0:T(8,128)S(1)}, u32[]{:S(2)}, u32[]{:S(2)}) collective-permute-start(f32[384,2048]{1,0:T(8,128)S(1)} %get-tuple-element.114), channel_id=1, source_target_pairs={{2,0},{3,1},{4,2},{5,3},{6,4},{7,5},{8,6},{9,7},{10,8},{11,9},{12,... | collective-permute-start | bytes 9437192 | tf_op jit(solution)/shard_map/ppermute | solution.py:22
Sparse Core Ops, SparseCore 0:
  13.8 97.7 all-reduce.2
  514.1 103.3 all-reduce.4
where the time goes:
time: 631 us; the launch traced here: 628 us
  waiting for transfers between devices  342 us (54%)
  matrix products  140 us (22%)
  other arithmetic  57.2 us (9%)
  local copies, waits for them, and re-layouts  50.6 us (8%)
  loops' own time  16.4 us (3%)
  between operations  13.5 us (2%)
  starting transfers between devices  9.26 us (1%)
    ppermute x4, waiting for transfers between devices, shifted(): lax.ppermute(value, axis, [(source, source + steps) for source in range(l...  140 us
    psum x1, waiting for transfers between devices, on_device(): return lax.psum(summed, 'section')  104 us
    psum x1, waiting for transfers between devices, spread(): return lax.psum(kept, axis)  97.9 us
    dot_general x24, matrix products, piece_grads(): jnp.einsum('aqk,qah->kh', grad_score, query_group, preferred_element_type...  55.7 us
    dot_general x24, matrix products, piece_attend(): jnp.einsum('aqk,kh->qah', weight_part, value_part, preferred_element_type...  37.8 us
    dot_general x24, matrix products, piece_scores(): jnp.einsum('qah,kh->aqk', query_group, key_part, preferred_element_type=j...  36.8 us
    convert_element_type x8, other arithmetic, group_grads(): attn_half = attn_weight.astype(jnp.bfloat16)  29.6 us
    another operation x1, loops' own time, on_device(): lax.map(group_grads, jnp.arange(shared_key_heads, dtype=jnp.int32))  16.4 us
  transfers between devices with their start and end apart: 6, of which 6 were waited for; matrix products, arithmetic and copies ran while one was open for 1% of the time, Pallas kernels for 0%

commit v1 on v0

--- a/solution.py
+++ b/solution.py
@@ -13,7 +13,7 @@
 
 def spread(value, axis, source):
     kept = jnp.where(lax.axis_index(axis) == source, value, 0).astype(value.dtype)
-    return lax.psum(kept, axis)
+    return jnp.sum(lax.all_gather(kept, axis), axis=0)
 
 
 def shifted(value, axis, steps):

time: 631 us -> 699 us (1.11)
  waiting for transfers between devices: 342 us -> 400 us
  other arithmetic: 57.2 us -> 68.3 us
    all_gather x0 -> x1, waiting for transfers between devices: none -> 155 us  [spread(): return jnp.sum(lax.all_gather(kept, axis), axis=0)]
    psum x1 -> x0, waiting for transfers between devices: 97.9 us -> none  [spread(): return lax.psum(kept, axis)]
    reduce_sum x0 -> x1, other arithmetic: none -> 9.2 us  [spread(): return jnp.sum(lax.all_gather(kept, axis), axis=0)]
where the time goes in v1:
time: 699 us; the launch traced here: 696 us
  waiting for transfers between devices  400 us (57%)
  matrix products  139 us (20%)
  other arithmetic  68.3 us (10%)
  local copies, waits for them, and re-layouts  49.9 us (7%)
  loops' own time  16.4 us (2%)
  between operations  13.5 us (2%)
  starting transfers between devices  9.57 us (1%)
    all_gather x1, waiting for transfers between devices, spread(): return jnp.sum(lax.all_gather(kept, axis), axis=0)  155 us
    ppermute x4, waiting for transfers between devices, shifted(): lax.ppermute(value, axis, [(source, source + steps) for source in range(l...  142 us
    psum x1, waiting for transfers between devices, on_device(): return lax.psum(summed, 'section')  103 us
    dot_general x24, matrix products, piece_grads(): jnp.einsum('aqk,qah->kh', grad_score, query_group, preferred_element_type...  54.8 us
    dot_general x24, matrix products, piece_attend(): jnp.einsum('aqk,kh->qah', weight_part, value_part, preferred_element_type...  37.9 us
    dot_general x24, matrix products, piece_scores(): jnp.einsum('qah,kh->aqk', query_group, key_part, preferred_element_type=j...  36.8 us
    convert_element_type x8, other arithmetic, group_grads(): attn_half = attn_weight.astype(jnp.bfloat16)  29.6 us
    another operation x1, loops' own time, on_device(): lax.map(group_grads, jnp.arange(shared_key_heads, dtype=jnp.int32))  16.4 us
  transfers between devices with their start and end apart: 6, of which 6 were waited for; matrix products, arithmetic and copies ran while one was open for 1% of the time, Pallas kernels for 0%

profile of v1, /device:TPU:32, one launch (start us, length us, event | category | flops | bytes accessed | tf_op | source)
XLA Modules:
  0.0 696.4 jit_solution(5229840966965574186)
XLA Ops:
  6.5 2.7 slice_select_fusion
  9.3 155.4 %all-gather.3.cloned.1.call-done = bf16[3072,2048]{1,0:T(8,128)(2,1)} async-done(((bf16[384,2048]{1,0:T(8,128)(2,1)}), bf16[3072,2048]{1,0:T(8,128)(2,1)}) %all-gather.3.cloned.1.call-update) | async-done | bytes 12582928 | tf_op jit(solution)/shard_map/all_gather | solution.py:16
  164.6 9.2 %reduce_sum.50 = bf16[384,2048]{1,0:T(8,128)(2,1)} reduce(bf16[8,384,2048]{2,1,0:T(8,128)(2,1)} %bitcast.257, bf16[]{:T(256)} %constant.52.clone.1), dimensions={0}, to_apply=%region_0.1 | reduce | flops 5505024 | bytes 14155778 | tf_op jit(solution)/shard_map/reduce_sum | solution.py:16
  173.8 3.6 collective-permute-start
  179.6 2.5 copy.74
  182.3 4.4 copy.75
  188.9 24.5 %collective-permute-done = bf16[384,2048]{1,0:T(8,128)(2,1)} collective-permute-done((bf16[384,2048]{1,0:T(8,128)(2,1)}, bf16[384,2048]{1,0:T(8,128)(2,1)}, u32[]{:S(2)}, u32[]{:S(2)}) %collective-permute-start) | collective-permute-done | bytes 1572896 | tf_op jit(solution)/shard_map/ppermute | solution.py:22
  213.4 15.0 %collective-permute-done.1 = bf16[384,2048]{1,0:T(8,128)(2,1)} collective-permute-done((bf16[384,2048]{1,0:T(8,128)(2,1)}, bf16[384,2048]{1,0:T(8,128)(2,1)}, u32[]{:S(2)}, u32[]{:S(2)}) %collective-permute-start.1) | collective-permute-done | bytes 1572896 | tf_op jit(solution)/shard_map/ppermute | solution.py:22
  233.3 2.6 copy.73
  235.9 223.8 %while.12 = (s32[]{:T(128)}, f32[8,1152,128]{2,1,0:T(8,128)}, f32[8,1152,128]{2,1,0:T(8,128)}, pred[384,1152]{0,1:T(8,128)(4,1)}, s32[8]{0:T(128)S(1)}, /*index=...) while((s32[]{:T(128)}, f32[8,1152,128]{2,1,0:T(8,128)}, ...), condition=%wide.region_10.11_spmd, body=%wide.region_4.10_spmd.sunk | while | flops 1720070784 | bytes 68940056 | solution.py:124
  244.9 3.7 fusion.120
  256.9 2.4 fusion.124
  272.9 3.7 fusion.120
  284.9 2.4 fusion.124
  300.9 3.7 fusion.120
  312.8 2.4 fusion.124
  328.9 3.7 fusion.120
  340.9 2.4 fusion.124
  356.9 3.7 fusion.120
  368.8 2.4 fusion.124
  384.9 3.7 fusion.120
  396.8 2.4 fusion.124
  412.8 3.7 fusion.120
  424.8 2.4 fusion.124
  440.8 3.7 fusion.120
  459.7 8.7 %copy_bitcast_fusion = (f32[1152,1024]{1,0:T(8,128)}, f32[1152,1024]{1,0:T(8,128)}) fusion(f32[8,1152,128]{2,1,0:T(8,128)} %get-tuple-element.53, f32[8,1152,128]{2,1,0:T(8,128)} %get-tuple-element.54), kind=kLoop, calls=%fused_computation.83 | loop fusion | bytes 18874368 | tf_op jit(solution)/shard_map/reshape | solution.py:127
  468.4 4.9 maximum_multiply_fusion
  477.9 64.8 %collective-permute-done.2 = f32[384,2048]{1,0:T(8,128)S(1)} collective-permute-done((f32[384,2048]{1,0:T(8,128)S(1)}, f32[384,2048]{1,0:T(8,128)S(1)}, u32[]{:S(2)}, u32[]{:S(2)}) %collective-permute-start.2) | collective-permute-done | bytes 3145760 | tf_op jit(solution)/shard_map/ppermute | solution.py:22
  542.7 37.5 %collective-permute-done.3 = f32[384,2048]{1,0:T(8,128)S(1)} collective-permute-done((f32[384,2048]{1,0:T(8,128)S(1)}, f32[384,2048]{1,0:T(8,128)S(1)}, u32[]{:S(2)}, u32[]{:S(2)}) %collective-permute-start.3) | collective-permute-done | bytes 3145760 | tf_op jit(solution)/shard_map/ppermute | solution.py:22
  580.1 2.7 fusion.63
  582.8 102.8 %all-reduce.2.cloned.1.call-done = f32[384,2048]{1,0:T(8,128)} async-done(((f32[384,2048]{1,0:T(8,128)}), f32[384,2048]{1,0:T(8,128)}) %all-reduce.2.cloned.1.call-update) | async-done | bytes 3145744 | tf_op jit(solution)/shard_map/psum | solution.py:134
  685.7 3.9 copy.121
  (206 shorter events, 175.3 us)
Async XLA Ops:
  6.5 158.1 %all-gather.3.cloned.1.call-start = ((), (), s32[]{:S(2)}) async-start(), calls=%async_computation.1 | async-start | bytes 14155776 | tf_op jit(solution)/shard_map/all_gather | solution.py:16
  9.2 676.5 %all-reduce.2.cloned.1.call-start = ((), (), s32[]{:S(2)}) async-start(), calls=%async_computation | async-start | bytes 6291456 | tf_op jit(solution)/shard_map/psum | solution.py:134
  164.6 14.9 %copy-start.2 = (bf16[1,384,3072]{2,1,0:T(8,128)(2,1)S(1)}, bf16[1,384,3072]{2,1,0:T(8,128)(2,1)}, u32[]{:S(2)}) copy-start(bf16[1,384,3072]{2,1,0:T(8,128)(2,1)} %param.5) | copy-start | bytes 7077892
  173.8 8.2 %copy-start.4 = (s32[31]{0:T(128)S(1)}, s32[31]{0:T(128)}, u32[]{:S(2)}) copy-start(s32[31]{0:T(128)} %param.7) | copy-start | bytes 376
  173.8 39.6 %collective-permute-start = (bf16[384,2048]{1,0:T(8,128)(2,1)}, bf16[384,2048]{1,0:T(8,128)(2,1)}, u32[]{:S(2)}, u32[]{:S(2)}) collective-permute-start(bf16[384,2048]{1,0:T(8,128)(2,1)} %reduce_sum.50), channel_id=1, source_target_pairs={{0,2},{1,3},{2,4},{3,5},{4,6},{5,7},{6,8},{7,9},{8,10},{9,11},{10,... | collective-permute-start | bytes 4718600 | tf_op jit(solution)/shard_map/ppermute | solution.py:22
  177.4 51.0 %collective-permute-start.1 = (bf16[384,2048]{1,0:T(8,128)(2,1)}, bf16[384,2048]{1,0:T(8,128)(2,1)}, u32[]{:S(2)}, u32[]{:S(2)}) collective-permute-start(bf16[384,2048]{1,0:T(8,128)(2,1)} %reduce_sum.50), channel_id=1, source_target_pairs={{0,1},{1,2},{2,3},{3,4},{4,5},{5,6},{6,7},{7,8},{8,9},{9,10},{10,1... | collective-permute-start | bytes 4718600 | tf_op jit(solution)/shard_map/ppermute | solution.py:22
  182.0 46.4 %copy-start.3 = (bf16[384,2048]{1,0:T(8,128)(2,1)S(1)}, bf16[384,2048]{1,0:T(8,128)(2,1)}, u32[]{:S(2)}) copy-start(bf16[384,2048]{1,0:T(8,128)(2,1)} %reduce_sum.50) | copy-start | bytes 4718596
  248.6 1.5 copy-start
  256.9 4.6 copy-start.1
  276.6 1.5 copy-start
  284.8 4.6 copy-start.1
  304.6 1.5 copy-start
  312.8 4.6 copy-start.1
  332.6 1.5 copy-start
  340.8 4.6 copy-start.1
  360.6 1.5 copy-start
  368.8 4.6 copy-start.1
  388.6 1.5 copy-start
  396.8 4.6 copy-start.1
  416.5 1.5 copy-start
  424.8 4.6 copy-start.1
  444.5 1.5 copy-start
  452.8 4.6 copy-start.1
  474.0 68.7 %collective-permute-start.2 = (f32[384,2048]{1,0:T(8,128)S(1)}, f32[384,2048]{1,0:T(8,128)S(1)}, u32[]{:S(2)}, u32[]{:S(2)}) collective-permute-start(f32[384,2048]{1,0:T(8,128)S(1)} %get-tuple-element.122), channel_id=1, source_target_pairs={{1,0},{2,1},{3,2},{4,3},{5,4},{6,5},{7,6},{8,7},{9,8},{10,9},{11,1... | collective-permute-start | bytes 9437192 | tf_op jit(solution)/shard_map/ppermute | solution.py:22
  476.0 104.2 %collective-permute-start.3 = (f32[384,2048]{1,0:T(8,128)S(1)}, f32[384,2048]{1,0:T(8,128)S(1)}, u32[]{:S(2)}, u32[]{:S(2)}) collective-permute-start(f32[384,2048]{1,0:T(8,128)S(1)} %get-tuple-element.123), channel_id=1, source_target_pairs={{2,0},{3,1},{4,2},{5,3},{6,4},{7,5},{8,6},{9,7},{10,8},{11,9},{12,... | collective-permute-start | bytes 9437192 | tf_op jit(solution)/shard_map/ppermute | solution.py:22
Sparse Core Ops, SparseCore 0:
  9.9 154.6 all-gather.2
  583.0 102.6 all-reduce.1
